TPU v7x, 512 devices: a whole 4x4x16 slice. The times are simulated.
512 devices in a mesh: hid: 64 (over y, x, z_hi, core), mod: 8 (over z_lo).
Axes of the slice: x: 4, y: 4, z: 16 (z_hi: 2, z_lo: 8; z = z_hi * 8 + z_lo), core: 2. Of those that a mesh axis runs over, the one named last changes fastest.
Arguments:
- tokens: bfloat16 [512, 8192], P('hid', 'mod'), may hold values from -6 to 6
- cotangent: bfloat16 [512, 8192], P('hid', 'mod'), may hold values from -1.2578125 to 1.2578125
- gate_weight: bfloat16 [8192, 26624], P('mod', 'hid'), may hold values from -0.0625 to 0.0625
- up_weight: bfloat16 [8192, 26624], P('mod', 'hid'), may hold values from -0.0625 to 0.0625
- down_weight: bfloat16 [26624, 8192], P('hid', 'mod'), may hold values from -0.0390625 to 0.0390625
Outputs:
- grad_in: bfloat16 [512, 8192], P('hid', 'mod')
- grad_gate: bfloat16 [8192, 26624], P('mod', 'hid')
- grad_up: bfloat16 [8192, 26624], P('mod', 'hid')
- grad_down: bfloat16 [26624, 8192], P('hid', 'mod')
All inputs are finite; a program needn't handle non-finite values.
Results may differ from a plain program's by a relative error of at most 0.027.
Values may be sent and summed in bfloat16 or wider, within the bound.
A program may use at most 64 MiB of HBM per device.

v0:
```python
import jax
import jax.numpy as jnp
from jax import lax
from jax.sharding import PartitionSpec as P

readout_scale = 2.0


def contract_last(left, right):
    return lax.dot_general(
        left, right, (((1,), (1,)), ((), ())), preferred_element_type=jnp.float32
    )


def contract_first(left, right):
    return lax.dot_general(
        left, right, (((0,), (0,)), ((), ())), preferred_element_type=jnp.float32
    )


def swiglu_grads(gate, up, back):
    back = readout_scale * back
    sigmoid_gate = jax.nn.sigmoid(gate)
    activated = gate * sigmoid_gate
    hidden = (activated * up).astype(jnp.bfloat16)
    d_gate = (back * up * sigmoid_gate * (1.0 + gate * (1.0 - sigmoid_gate))).astype(jnp.bfloat16)
    d_up = (back * activated).astype(jnp.bfloat16)
    return (hidden, d_gate, d_up)


def local(tokens, cotangent, gate_weight, up_weight, down_weight):
    piece = lax.all_gather(tokens, "hid", axis=0, tiled=True)
    token_rows = piece
    gate_part = jnp.dot(piece, gate_weight, preferred_element_type=jnp.float32)
    up_part = jnp.dot(piece, up_weight, preferred_element_type=jnp.float32)
    piece = lax.all_gather(cotangent, "hid", axis=0, tiled=True)
    back_part = contract_last(piece, down_weight)
    gate_sum, up_sum, back_sum = (
        lax.psum(gate_part.astype(jnp.bfloat16), "mod").astype(jnp.float32),
        lax.psum(up_part.astype(jnp.bfloat16), "mod").astype(jnp.float32),
        lax.psum(back_part.astype(jnp.bfloat16), "mod").astype(jnp.float32),
    )
    hidden, d_gate, d_up = swiglu_grads(gate_sum, up_sum, back_sum)
    grad_down = (readout_scale * contract_first(hidden, piece)).astype(jnp.bfloat16)
    grad_gate = contract_first(token_rows, d_gate).astype(jnp.bfloat16)
    grad_up = contract_first(token_rows, d_up).astype(jnp.bfloat16)
    grad_in = lax.psum_scatter(
        contract_last(d_gate, gate_weight) + contract_last(d_up, up_weight),
        "hid",
        scatter_dimension=0,
        tiled=True,
    ).astype(jnp.bfloat16)
    return (grad_in, grad_gate, grad_up, grad_down)


def solution(mesh):
    placed = (P("hid", "mod"), P("hid", "mod"), P("mod", "hid"), P("mod", "hid"), P("hid", "mod"))
    return jax.shard_map(
        local,
        mesh=mesh,
        in_specs=placed,
        out_specs=(P("hid", "mod"), P("mod", "hid"), P("mod", "hid"), P("hid", "mod")),
        check_vma=False,
    )
```

profile of v0, /device:TPU:32, one launch (start us, length us, event | category | flops | bytes accessed | tf_op | source)
XLA Modules:
  0.0 922.5 jit_solution(11970317265629496496)
XLA Ops:
  7.2 0.0 copy-start
  7.2 0.0 all-gather.5.cloned.1.call-start
  7.2 0.7 all-gather.5.cloned.1.call-update
  7.9 0.0 all-gather.3.cloned.1.call-start
  8.0 0.7 all-gather.3.cloned.1.call-update
  8.7 0.0 all-reduce.3.cloned.1.call-start
  8.7 104.6 %all-gather.5.cloned.1.call-done = bf16[512,1024]{1,0:T(8,128)(2,1)} async-done(((bf16[8,1024]{1,0:T(8,128)(2,1)}), bf16[512,1024]{1,0:T(8,128)(2,1)}) %all-gather.5.cloned.1.call-update) | async-done | bytes 1048592 | tf_op jit(solution)/shard_map/all_gather | solution.py:32
  113.3 0.0 copy-done
  113.3 0.0 copy-start.1
  113.3 0.0 copy-start.4
  113.3 2.8 convolution_convert_fusion.2
  116.0 0.0 copy-done.1
  116.1 0.0 copy-done.4
  116.1 0.0 copy-start.3
  116.1 1.4 convolution_convert_fusion.3
  117.5 92.6 %all-gather.3.cloned.1.call-done = bf16[512,1024]{1,0:T(8,128)(2,1)} async-done(((bf16[8,1024]{1,0:T(8,128)(2,1)}), bf16[512,1024]{1,0:T(8,128)(2,1)}) %all-gather.3.cloned.1.call-update) | async-done | bytes 1048592 | tf_op jit(solution)/shard_map/all_gather | solution.py:36
  210.1 0.0 copy-done.3
  210.1 2.6 convolution_convert_fusion.4
  212.7 0.0 all-reduce.3.cloned.1.call-update
  212.7 0.0 reduce-scatter.2.cloned.1.call-start
  212.8 121.7 %all-reduce.3.cloned.1.call-done = (bf16[512,416]{0,1:T(8,128)(2,1)}, bf16[512,416]{0,1:T(8,128)(2,1)}, bf16[512,416]{0,1:T(8,128)(2,1)}) async-done(((bf16[512,416]{0,1:T(8,128)(2,1)}, bf16[512,416]{0,1:T(8,128)(2,1)}, bf16[512,416]{0,1:T(8,128)(2,1)}), (bf16[512,416]{0,1:T(8,128)(2,1)}, bf16[512,416]{0,1:T(8,128)(2,1)}, bf16[512,416]{0,1:T(8,128)(2,1)})) %all-reduce.3.cloned.1.call-update) | async-done | bytes 1277968 | tf_op jit(solution)/shard_map/psum | solution.py:40
  334.5 0.0 copy-start.5
  334.5 0.0 copy-start.7
  334.5 0.0 copy-start.8
  334.5 2.3 fusion.13
  336.9 0.0 copy-done.5
  336.9 0.0 copy-done.7
  336.9 0.0 copy-done.8
  336.9 2.2 convolution_add_fusion
  339.1 0.0 reduce-scatter.2.cloned.1.call-update
  339.1 0.0 copy-start.2
  339.1 0.0 copy-start.6
  339.1 1.6 fusion.1
  340.7 0.0 copy-done.2
  340.7 0.0 copy-done.6
  340.7 1.6 multiply_convert_fusion
  342.3 1.7 fusion
  344.0 570.5 %reduce-scatter.2.cloned.1.call-done = f32[8,1024]{1,0:T(8,128)} async-done(((f32[512,1024]{1,0:T(8,128)}), f32[8,1024]{1,0:T(8,128)}) %reduce-scatter.2.cloned.1.call-update) | async-done | bytes 32784 | tf_op jit(solution)/shard_map/reduce_scatter | solution.py:47
  914.6 1.4 convert_element_type.53
Async XLA Ops:
  7.2 106.1 %copy-start = (bf16[1024,416]{0,1:T(8,128)(2,1)S(1)}, bf16[1024,416]{0,1:T(8,128)(2,1)}, u32[]{:S(2)}) copy-start(bf16[1024,416]{0,1:T(8,128)(2,1)} %param.7) | copy-start | bytes 2555908
  7.2 106.1 %all-gather.5.cloned.1.call-start = ((), (), s32[]{:S(2)}) async-start(), calls=%async_computation.2 | async-start | bytes 1064960 | tf_op jit(solution)/shard_map/all_gather | solution.py:32
  7.9 202.2 %all-gather.3.cloned.1.call-start = ((), (), s32[]{:S(2)}) async-start(), calls=%async_computation.1 | async-start | bytes 1064960 | tf_op jit(solution)/shard_map/all_gather | solution.py:36
  8.7 325.9 %all-reduce.3.cloned.1.call-start = ((), (), s32[]{:S(2)}) async-start(), calls=%async_computation.4 | async-start | bytes 2555904 | tf_op jit(solution)/shard_map/psum | solution.py:40
  113.3 2.8 copy-start.1
  113.3 2.8 copy-start.4
  116.1 94.0 %copy-start.3 = (bf16[416,1024]{1,0:T(8,128)(2,1)S(1)}, bf16[416,1024]{1,0:T(8,128)(2,1)}, u32[]{:S(2)}) copy-start(bf16[416,1024]{1,0:T(8,128)(2,1)} %param.9) | copy-start | bytes 2555908
  212.7 701.8 %reduce-scatter.2.cloned.1.call-start = ((), (), s32[]{:S(2)}) async-start(), calls=%async_computation.3 | async-start | bytes 2129920 | tf_op jit(solution)/shard_map/reduce_scatter | solution.py:47
  334.5 2.3 copy-start.5
  334.5 2.4 copy-start.7
  334.5 2.4 copy-start.8
  339.1 1.6 copy-start.2
  339.1 1.6 copy-start.6
Sparse Core Ops, SparseCore 0:
  12.4 100.8 all-gather.4
  117.6 92.4 all-gather.2
  213.8 120.6 all-reduce.2
  339.2 575.2 reduce-scatter.1
where the time goes:
time: 923 us; the launch traced here: 922 us
  waiting for transfers between devices  891 us (97%)
  matrix products  16.2 us (2%)
  between operations  13.8 us (1%)
    reduce_scatter x1, waiting for transfers between devices, local(): lax.psum_scatter(contract_last(d_gate, gate_weight) + contract_last(d_up,...  571 us
    psum x1, waiting for transfers between devices, local(): lax.psum(up_part.astype(jnp.bfloat16), 'mod').astype(jnp.float32)  122 us
    all_gather x1, waiting for transfers between devices, local(): piece = lax.all_gather(tokens, 'hid', axis=0, tiled=True)  105 us
    all_gather x1, waiting for transfers between devices, local(): piece = lax.all_gather(cotangent, 'hid', axis=0, tiled=True)  92.6 us
  transfers between devices with their start and end apart: 4, of which 4 were waited for; matrix products, arithmetic and copies ran while one was open for 1% of the time, Pallas kernels for 0%

commit v1 on v0

--- a/solution.py
+++ b/solution.py
@@ -29,7 +29,9 @@
 
 
 def local(tokens, cotangent, gate_weight, up_weight, down_weight):
-    piece = lax.all_gather(tokens, "hid", axis=0, tiled=True)
+    piece = jnp.concatenate(
+        lax.all_to_all(jnp.stack([tokens] * lax.axis_size("hid")), "hid", 0, 0), axis=0
+    )
     token_rows = piece
     gate_part = jnp.dot(piece, gate_weight, preferred_element_type=jnp.float32)
     up_part = jnp.dot(piece, up_weight, preferred_element_type=jnp.float32)

time: 923 us -> 865 us (0.937)
  waiting for transfers between devices: 891 us -> 811 us
  starting transfers between devices: 0.16 us -> 20.4 us
    all_gather x1 -> x0, waiting for transfers between devices: 105 us -> none  [local(): piece = lax.all_gather(tokens, 'hid', axis=0, tiled=True)]
    all_gather x1, waiting for transfers between devices: 92.6 us -> 118 us  [local(): piece = lax.all_gather(cotangent, 'hid', axis=0, tiled=True)]
    all_to_all x0 -> x1, starting transfers between devices: none -> 20.3 us  [local(): lax.all_to_all(jnp.stack([tokens] * lax.axis_size('hid')), 'hid', 0, 0)]
  transfers between devices with their start and end apart: 4 -> 4, of which waited for: 4 -> 3; matrix products, arithmetic and copies ran while one was open for 1% -> 1% of each run, Pallas kernels for 0% -> 0%
where the time goes in v1:
time: 865 us; the launch traced here: 864 us
  waiting for transfers between devices  811 us (94%)
  starting transfers between devices  20.4 us (2%)
  matrix products  16 us (2%)
  between operations  13.8 us (2%)
    reduce_scatter x1, waiting for transfers between devices, local(): lax.psum_scatter(contract_last(d_gate, gate_weight) + contract_last(d_up,...  571 us
    psum x1, waiting for transfers between devices, local(): lax.psum(up_part.astype(jnp.bfloat16), 'mod').astype(jnp.float32)  120 us
    all_gather x1, waiting for transfers between devices, local(): piece = lax.all_gather(cotangent, 'hid', axis=0, tiled=True)  118 us
    all_to_all x1, starting transfers between devices, local(): lax.all_to_all(jnp.stack([tokens] * lax.axis_size('hid')), 'hid', 0, 0)  20.3 us
  transfers between devices with their start and end apart: 4, of which 3 were waited for; matrix products, arithmetic and copies ran while one was open for 1% of the time, Pallas kernels for 0%

profile of v1, /device:TPU:32, one launch (start us, length us, event | category | flops | bytes accessed | tf_op | source)
XLA Modules:
  0.0 864.2 jit_solution(8224992569209504013)
XLA Ops:
  7.2 0.0 copy-start
  7.2 0.0 copy-start.2
  7.2 1.9 stack.2
  9.1 20.3 %all-to-all-start = ((bf16[64,8,1024]{2,1,0:T(8,128)(2,1)}), bf16[64,8,1024]{2,1,0:T(8,128)(2,1)S(1)}, u32[]{:S(2)}, u32[]{:S(2)}) async-start(bf16[64,8,1024]{2,1,0:T(8,128)(2,1)} %stack.2), calls=%async_computation | async-start | bytes 2097152 | tf_op jit(solution)/shard_map/all_to_all | solution.py:33
  29.4 0.0 all-gather.2.cloned.1.call-start
  29.5 0.7 all-gather.2.cloned.1.call-update
  30.2 0.0 all-reduce.3.cloned.1.call-start
  30.2 118.3 %all-gather.2.cloned.1.call-done = bf16[512,1024]{1,0:T(8,128)(2,1)} async-done(((bf16[8,1024]{1,0:T(8,128)(2,1)}), bf16[512,1024]{1,0:T(8,128)(2,1)}) %all-gather.2.cloned.1.call-update) | async-done | bytes 1048592 | tf_op jit(solution)/shard_map/all_gather | solution.py:38
  148.5 0.0 copy-done.2
  148.5 2.6 convolution_convert_fusion.4
  151.1 0.0 all-to-all-done
  151.1 2.6 convolution_convert_fusion.3
  153.7 0.0 copy-done
  153.7 1.4 convolution_convert_fusion.2
  155.1 0.0 all-reduce.3.cloned.1.call-update
  155.1 0.0 reduce-scatter.2.cloned.1.call-start
  155.2 120.4 %all-reduce.3.cloned.1.call-done = (bf16[512,416]{0,1:T(8,128)(2,1)}, bf16[512,416]{0,1:T(8,128)(2,1)}, bf16[512,416]{0,1:T(8,128)(2,1)}) async-done(((bf16[512,416]{0,1:T(8,128)(2,1)}, bf16[512,416]{0,1:T(8,128)(2,1)}, bf16[512,416]{0,1:T(8,128)(2,1)}), (bf16[512,416]{0,1:T(8,128)(2,1)}, bf16[512,416]{0,1:T(8,128)(2,1)}, bf16[512,416]{0,1:T(8,128)(2,1)})) %all-reduce.3.cloned.1.call-update) | async-done | bytes 1277968 | tf_op jit(solution)/shard_map/psum | solution.py:42
  275.6 0.0 copy-start.3
  275.6 0.0 copy-start.5
  275.6 0.0 copy-start.6
  275.6 2.3 fusion.17
  277.9 0.0 copy-done.3
  277.9 0.0 copy-done.5
  278.0 0.0 copy-done.6
  278.0 2.2 convolution_add_fusion
  280.1 0.0 reduce-scatter.2.cloned.1.call-update
  280.2 0.0 copy-start.1
  280.2 0.0 copy-start.4
  280.2 1.6 fusion.1
  281.8 0.0 copy-done.1
  281.8 0.0 copy-done.4
  281.8 1.6 multiply_convert_fusion
  283.4 1.7 fusion
  285.1 571.2 %reduce-scatter.2.cloned.1.call-done = f32[8,1024]{1,0:T(8,128)} async-done(((f32[512,1024]{1,0:T(8,128)}), f32[8,1024]{1,0:T(8,128)}) %reduce-scatter.2.cloned.1.call-update) | async-done | bytes 32784 | tf_op jit(solution)/shard_map/reduce_scatter | solution.py:49
  856.4 1.4 convert_element_type.53
Async XLA Ops:
  7.2 146.5 %copy-start = (bf16[1024,416]{0,1:T(8,128)(2,1)S(1)}, bf16[1024,416]{0,1:T(8,128)(2,1)}, u32[]{:S(2)}) copy-start(bf16[1024,416]{0,1:T(8,128)(2,1)} %param.7) | copy-start | bytes 2555908
  7.2 141.3 %copy-start.2 = (bf16[416,1024]{1,0:T(8,128)(2,1)S(1)}, bf16[416,1024]{1,0:T(8,128)(2,1)}, u32[]{:S(2)}) copy-start(bf16[416,1024]{1,0:T(8,128)(2,1)} %param.9) | copy-start | bytes 2555908
  9.1 142.0 %all-to-all-start = ((bf16[64,8,1024]{2,1,0:T(8,128)(2,1)}), bf16[64,8,1024]{2,1,0:T(8,128)(2,1)S(1)}, u32[]{:S(2)}, u32[]{:S(2)}) async-start(bf16[64,8,1024]{2,1,0:T(8,128)(2,1)} %stack.2), calls=%async_computation | async-start | bytes 2097152 | tf_op jit(solution)/shard_map/all_to_all | solution.py:33
  29.4 119.1 %all-gather.2.cloned.1.call-start = ((), (), s32[]{:S(2)}) async-start(), calls=%async_computation.2 | async-start | bytes 1064960 | tf_op jit(solution)/shard_map/all_gather | solution.py:38
  30.2 245.4 %all-reduce.3.cloned.1.call-start = ((), (), s32[]{:S(2)}) async-start(), calls=%async_computation.4 | async-start | bytes 2555904 | tf_op jit(solution)/shard_map/psum | solution.py:42
  155.1 701.2 %reduce-scatter.2.cloned.1.call-start = ((), (), s32[]{:S(2)}) async-start(), calls=%async_computation.3 | async-start | bytes 2129920 | tf_op jit(solution)/shard_map/reduce_scatter | solution.py:49
  275.6 2.3 copy-start.3
  275.6 2.4 copy-start.5
  275.6 2.4 copy-start.6
  280.2 1.6 copy-start.1
  280.2 1.6 copy-start.4
Sparse Core Ops, SparseCore 0:
  34.6 113.8 all-gather.1
  155.2 120.3 all-reduce.2
  280.3 576.0 reduce-scatter.1

commit v2 on v0

--- a/solution.py
+++ b/solution.py
@@ -37,7 +37,7 @@
     back_part = contract_last(piece, down_weight)
     gate_sum, up_sum, back_sum = (
         lax.psum(gate_part.astype(jnp.bfloat16), "mod").astype(jnp.float32),
-        lax.psum(up_part.astype(jnp.bfloat16), "mod").astype(jnp.float32),
+        jnp.sum(lax.all_gather(up_part.astype(jnp.bfloat16), "mod"), axis=0).astype(jnp.float32),
         lax.psum(back_part.astype(jnp.bfloat16), "mod").astype(jnp.float32),
     )
     hidden, d_gate, d_up = swiglu_grads(gate_sum, up_sum, back_sum)

time: 923 us -> 1000 us (1.083)
  waiting for transfers between devices: 891 us -> 965 us
    all_gather x0 -> x1, waiting for transfers between devices: none -> 78.6 us  [local(): lax.all_gather(up_part.astype(jnp.bfloat16), 'mod')]
  transfers between devices with their start and end apart: 4 -> 5, of which waited for: 4 -> 5; matrix products, arithmetic and copies ran while one was open for 1% -> 2% of each run, Pallas kernels for 0% -> 0%
where the time goes in v2:
time: 1000 us
  waiting for transfers between devices  965 us (96%)
  matrix products  16.3 us (2%)
  between operations  13.8 us (1%)
    reduce_scatter x1, waiting for transfers between devices, local(): lax.psum_scatter(contract_last(d_gate, gate_weight) + contract_last(d_up,...  571 us
    psum x1, waiting for transfers between devices, local(): lax.psum(gate_part.astype(jnp.bfloat16), 'mod').astype(jnp.float32)  117 us
    all_gather x1, waiting for transfers between devices, local(): piece = lax.all_gather(tokens, 'hid', axis=0, tiled=True)  105 us
    all_gather x1, waiting for transfers between devices, local(): piece = lax.all_gather(cotangent, 'hid', axis=0, tiled=True)  92.3 us
    all_gather x1, waiting for transfers between devices, local(): lax.all_gather(up_part.astype(jnp.bfloat16), 'mod')  78.6 us
  transfers between devices with their start and end apart: 5, of which 5 were waited for; matrix products, arithmetic and copies ran while one was open for 2% of the time, Pallas kernels for 0%

profile of v2, /device:TPU:32, one launch (start us, length us, event | category | flops | bytes accessed | tf_op | source)
XLA Modules:
  0.0 1002.9 jit_solution(9768891489685259752)
XLA Ops:
  7.2 0.0 copy-start
  7.2 0.0 all-gather.7.cloned.1.call-start
  7.2 0.7 all-gather.7.cloned.1.call-update
  7.9 0.0 all-gather.5.cloned.1.call-start
  8.0 0.7 all-gather.5.cloned.1.call-update
  8.7 0.0 all-gather.9.cloned.1.call-start
  8.7 104.6 %all-gather.7.cloned.1.call-done = bf16[512,1024]{1,0:T(8,128)(2,1)} async-done(((bf16[8,1024]{1,0:T(8,128)(2,1)}), bf16[512,1024]{1,0:T(8,128)(2,1)}) %all-gather.7.cloned.1.call-update) | async-done | bytes 1048592 | tf_op jit(solution)/shard_map/all_gather | solution.py:32
  113.3 0.0 copy-start.1
  113.3 3.0 convolution_convert_fusion.3
  116.2 0.0 copy-start.3
  116.2 0.0 all-gather.9.cloned.1.call-update
  116.3 0.0 all-reduce.3.cloned.1.call-start
  116.3 0.0 copy-done
  116.3 0.0 copy-done.1
  116.3 1.4 convolution_convert_fusion.2
  117.7 92.3 %all-gather.5.cloned.1.call-done = bf16[512,1024]{1,0:T(8,128)(2,1)} async-done(((bf16[8,1024]{1,0:T(8,128)(2,1)}), bf16[512,1024]{1,0:T(8,128)(2,1)}) %all-gather.5.cloned.1.call-update) | async-done | bytes 1048592 | tf_op jit(solution)/shard_map/all_gather | solution.py:36
  210.1 0.0 copy-done.3
  210.1 2.6 convolution_convert_fusion.4
  212.7 0.0 all-reduce.3.cloned.1.call-update
  212.7 0.0 reduce-scatter.2.cloned.1.call-start
  212.8 78.6 %all-gather.9.cloned.1.call-done = bf16[4096,416]{0,1:T(8,128)(2,1)} async-done(((bf16[512,416]{0,1:T(8,128)(2,1)}), bf16[4096,416]{0,1:T(8,128)(2,1)}) %all-gather.9.cloned.1.call-update) | async-done | bytes 3407888 | tf_op jit(solution)/shard_map/all_gather | solution.py:40
  291.4 3.8 copy.9
  295.1 2.5 bitcast_reduce_fusion
  297.6 117.3 %all-reduce.3.cloned.1.call-done = (bf16[512,416]{0,1:T(8,128)(2,1)}, bf16[512,416]{0,1:T(8,128)(2,1)}) async-done(((bf16[512,416]{0,1:T(8,128)(2,1)}, bf16[512,416]{0,1:T(8,128)(2,1)}), (bf16[512,416]{0,1:T(8,128)(2,1)}, bf16[512,416]{0,1:T(8,128)(2,1)})) %all-reduce.3.cloned.1.call-update) | async-done | bytes 851984 | tf_op jit(solution)/shard_map/psum | solution.py:39
  415.0 0.0 copy-start.4
  415.0 0.0 copy-start.5
  415.0 0.0 copy-start.6
  415.0 2.2 fusion.13
  417.2 0.0 copy-done.4
  417.2 0.0 copy-done.5
  417.2 0.0 copy-done.6
  417.2 2.2 convolution_add_fusion
  419.4 0.0 reduce-scatter.2.cloned.1.call-update
  419.4 0.0 copy-start.2
  419.4 1.6 fusion.1
  421.0 0.0 copy-done.2
  421.0 1.6 multiply_convert_fusion
  422.6 1.7 fusion
  424.4 570.6 %reduce-scatter.2.cloned.1.call-done = f32[8,1024]{1,0:T(8,128)} async-done(((f32[512,1024]{1,0:T(8,128)}), f32[8,1024]{1,0:T(8,128)}) %reduce-scatter.2.cloned.1.call-update) | async-done | bytes 32784 | tf_op jit(solution)/shard_map/reduce_scatter | solution.py:47
  995.0 1.4 convert_element_type.55
Async XLA Ops:
  7.2 109.2 %copy-start = (bf16[1024,416]{0,1:T(8,128)(2,1)S(1)}, bf16[1024,416]{0,1:T(8,128)(2,1)}, u32[]{:S(2)}) copy-start(bf16[1024,416]{0,1:T(8,128)(2,1)} %param.7) | copy-start | bytes 2555908
  7.2 106.1 %all-gather.7.cloned.1.call-start = ((), (), s32[]{:S(2)}) async-start(), calls=%async_computation.2 | async-start | bytes 1064960 | tf_op jit(solution)/shard_map/all_gather | solution.py:32
  7.9 202.2 %all-gather.5.cloned.1.call-start = ((), (), s32[]{:S(2)}) async-start(), calls=%async_computation.1 | async-start | bytes 1064960 | tf_op jit(solution)/shard_map/all_gather | solution.py:36
  8.7 282.7 %all-gather.9.cloned.1.call-start = ((), (), s32[]{:S(2)}) async-start(), calls=%async_computation.4 | async-start | bytes 3833856 | tf_op jit(solution)/shard_map/all_gather | solution.py:40
  113.3 3.0 copy-start.1
  116.2 93.8 %copy-start.3 = (bf16[416,1024]{1,0:T(8,128)(2,1)S(1)}, bf16[416,1024]{1,0:T(8,128)(2,1)}, u32[]{:S(2)}) copy-start(bf16[416,1024]{1,0:T(8,128)(2,1)} %param.9) | copy-start | bytes 2555908
  116.3 298.7 %all-reduce.3.cloned.1.call-start = ((), (), s32[]{:S(2)}) async-start(), calls=%async_computation.5 | async-start | bytes 1703936 | tf_op jit(solution)/shard_map/psum | solution.py:39
  212.7 782.3 %reduce-scatter.2.cloned.1.call-start = ((), (), s32[]{:S(2)}) async-start(), calls=%async_computation.3 | async-start | bytes 2129920 | tf_op jit(solution)/shard_map/reduce_scatter | solution.py:47
  415.0 2.2 copy-start.4
  415.0 2.2 copy-start.5
  415.0 2.2 copy-start.6
  419.4 1.6 copy-start.2
Sparse Core Ops, SparseCore 0:
  12.4 100.8 all-gather.6
  117.6 92.4 all-gather.4
  212.7 78.5 all-gather.8
  294.8 120.1 all-reduce.2
  419.5 575.4 reduce-scatter.1
